TPU v7x, 32 devices: a whole 2x2x4 slice. The times are simulated.
32 devices in a mesh: sub: 8 (over z, y), freq: 4 (over x, core).
Axes of the slice: x: 2, y: 2, z: 4, core: 2. Of those that a mesh axis runs over, the one named last changes fastest.
Arguments:
- freq_squared: float32 [16], P('freq'), may hold values from 0.05 to 1
- displacement: bfloat16 [1536, 2048], P('freq', 'sub'), may hold values from -6 to 6
- adjoint: bfloat16 [1536, 2048], P('freq', 'sub'), may hold values from -6 to 6
- incidence: int32 [24, 4], P('sub'), may hold values from 0 to 15, as said below
- block_count: int32 [24], P('sub'), may hold values from 1 to 4, as said below
- mode_count: int32 [24], P('sub'), may hold values from 1 to 128, as said below
- stiffness: bfloat16 [24, 512, 512], P('sub'), may hold values from -0.25 to 0.25
- mass_matrix: bfloat16 [24, 512, 512], P('sub'), may hold values from -0.25 to 0.25
- coupling: bfloat16 [24, 128, 512], P('sub'), may hold values from -0.25 to 0.25
- eigenvalues: float32 [24, 128], P('sub'), may hold values from 1.5 to 20
- flexibility: float32 [24, 512], P('sub'), may hold values from 0.2 to 1
Outputs:
- interface_residual: float32 [1536, 2048], P('freq', 'sub')
- eigen_gradient: float32 [24, 128], P('sub')
- coupling_gradient: float32 [24, 128, 512], P('sub', None, 'freq')
- flexibility_gradient: float32 [24, 512], P('sub')
Inputs may be any that keep to these rules, and one draw needn't show every extreme that they name: `incidence`: every slot, live or not, names a block owned by the index of sub that holds the substructure or one at most 1 indices away (block b is owned by index b // 2). The first substructure of every index of sub touches, in live slots, a block of the owner 1 indices below and one 1 above wherever such owners exist. A substructure may name one block in several slots. `block_count`: the first substructure of every index of sub has 4 live slots. Modes j >= mode_count[s] are absent. The first substructure of every index of sub keeps 128 modes.
All inputs are finite; a program needn't handle non-finite values.
Results may differ from a plain program's by a relative error of at most 0.0029.
Values may be sent and summed in bfloat16 or wider, within the bound.
A program may use at most 64 MiB of HBM per device.

v0:
```python
import jax
import jax.numpy as jnp
from jax import lax
from jax.sharding import PartitionSpec as P

WIN = 1


def extended(x, sides, width):
    for axis, dim in sides:
        devices, length = (lax.axis_size(axis), x.shape[dim])
        up = [(i, (i + 1) % devices) for i in range(devices - 1)]
        down = [(j, i) for i, j in up]
        last = lax.slice_in_dim(x, length - width, length, axis=dim)
        first = lax.slice_in_dim(x, 0, width, axis=dim)
        before = lax.ppermute(last, axis, up)
        after = lax.ppermute(first, axis, down)
        x = jnp.concatenate([before, x, after], axis=dim)
    return x


def from_behind(block, axis, distance):
    devices = range(lax.axis_size(axis))
    route = [(i - distance, i) for i in devices if i - distance in devices]
    return lax.ppermute(block, axis, route)


def shards(
    freq_squared,
    displacement,
    adjoint,
    incidence,
    block_count,
    mode_count,
    stiffness,
    mass_matrix,
    coupling,
    eigenvalues,
    flexibility,
):
    sub_here, slot_count = incidence.shape
    columns, owned_cells = displacement.shape
    block_size = stiffness.shape[1] // slot_count
    owned_blocks = owned_cells // block_size
    mode_width = coupling.shape[1]
    squares = jnp.repeat(freq_squared, columns // freq_squared.shape[0])
    fourth = squares * squares
    stacked = jnp.stack((adjoint, displacement))
    window = extended(stacked, (("sub", 2),), WIN * owned_blocks * block_size)
    window_blocks = window.shape[2] // block_size
    first_block = (lax.axis_index("sub") - WIN) * owned_blocks
    position = (incidence - first_block).reshape(-1)
    live_slot = (jnp.arange(slot_count)[None, :] < block_count[:, None]).reshape(-1)
    blocks = window.reshape(2, columns, window_blocks, block_size)
    picked = (
        jnp.take(blocks, position, axis=2) * live_slot.astype(jnp.bfloat16)[None, None, :, None]
    )
    picked = picked.reshape(2, columns, sub_here, slot_count * block_size)
    adjoint_sub = picked[0]
    displacement_sub = picked[1]
    modal_adjoint = jnp.einsum(
        "csk,smk->csm", adjoint_sub, coupling, preferred_element_type=jnp.float32
    )
    modal_displacement = jnp.einsum(
        "csk,smk->csm", displacement_sub, coupling, preferred_element_type=jnp.float32
    )
    mode_live = jnp.arange(mode_width)[None, :] < mode_count[:, None]
    inverse = 1.0 / (eigenvalues[None, :, :] - squares[:, None, None])
    factor = jnp.where(mode_live[None, :, :], fourth[:, None, None] * inverse, jnp.float32(0.0))
    weight_adjoint = (factor * modal_adjoint).astype(jnp.bfloat16)
    weight_displacement = (factor * modal_displacement).astype(jnp.bfloat16)
    eigen_part = jnp.sum(factor * inverse * modal_adjoint * modal_displacement, axis=0)
    flex_part = -jnp.sum(
        fourth[:, None, None]
        * adjoint_sub.astype(jnp.float32)
        * displacement_sub.astype(jnp.float32),
        axis=0,
    )
    eigen_gradient, flexibility_gradient = lax.psum((eigen_part, flex_part), "freq")
    response = (
        jnp.einsum("csk,sjk->csj", adjoint_sub, stiffness, preferred_element_type=jnp.float32)
        - squares[:, None, None]
        * jnp.einsum("csk,sjk->csj", adjoint_sub, mass_matrix, preferred_element_type=jnp.float32)
        - jnp.einsum("csm,smk->csk", weight_adjoint, coupling, preferred_element_type=jnp.float32)
        - fourth[:, None, None] * flexibility[None, :, :] * adjoint_sub.astype(jnp.float32)
    )
    selector = (
        (position[:, None] == jnp.arange(window_blocks)[None, :]) & live_slot[:, None]
    ).astype(jnp.float32)
    contribution = jnp.einsum(
        "cxb,xw->cwb",
        response.reshape(columns, sub_here * slot_count, block_size),
        selector,
        precision=lax.Precision.HIGHEST,
    )
    contribution = contribution.reshape(columns, window_blocks * block_size)
    slab_width = owned_blocks * block_size
    summed = contribution[:, WIN * slab_width : (WIN + 1) * slab_width]
    for offset in range(-WIN, WIN + 1):
        if offset != 0:
            owner_slab = contribution[
                :, (offset + WIN) * slab_width : (offset + WIN + 1) * slab_width
            ]
            summed = summed + from_behind(owner_slab, "sub", offset)
    partial_gradient = -(
        jnp.einsum(
            "csm,csk->smk", weight_adjoint, displacement_sub, preferred_element_type=jnp.float32
        )
        + jnp.einsum(
            "csm,csk->smk", weight_displacement, adjoint_sub, preferred_element_type=jnp.float32
        )
    )
    coupling_gradient = lax.psum_scatter(partial_gradient, "freq", scatter_dimension=2, tiled=True)
    return (summed, eigen_gradient, coupling_gradient, flexibility_gradient)


def solution(mesh):
    in_specs = (
        P("freq"),
        P("freq", "sub"),
        P("freq", "sub"),
        P("sub", None),
        P("sub"),
        P("sub"),
        P("sub", None, None),
        P("sub", None, None),
        P("sub", None, None),
        P("sub", None),
        P("sub", None),
    )
    out_specs = (P("freq", "sub"), P("sub", None), P("sub", None, "freq"), P("sub", None))
    return jax.shard_map(shards, mesh=mesh, in_specs=in_specs, out_specs=out_specs, check_vma=False)
```

profile of v0, /device:TPU:0, one launch (start us, length us, event | category | flops | bytes accessed | tf_op | source)
XLA Modules:
  0.0 102.3 jit_solution(13047086922342960374)
XLA Ops:
  9.6 1.3 %collective-permute-start.1 = (bf16[2,384,256]{1,2,0:T(8,128)(2,1)S(1)}, bf16[2,384,256]{1,2,0:T(8,128)(2,1)S(1)}, u32[]{:S(2)}, u32[]{:S(2)}) collective-permute-start(bf16[2,384,256]{1,2,0:T(8,128)(2,1)S(1)} %pad_maximum_fusion.1), channel_id=1, source_target_pairs={{4,0},{8,4},{12,8},{16,12},{20,16},{24,20},{28,24},{5,1},{9,5},{13... | collective-permute-start | bytes 1179656 | tf_op jit(solution)/shard_map/ppermute | solution.py:17
  10.9 5.6 %collective-permute-start = (bf16[2,384,256]{1,2,0:T(8,128)(2,1)S(1)}, bf16[2,384,256]{1,2,0:T(8,128)(2,1)S(1)}, u32[]{:S(2)}, u32[]{:S(2)}) collective-permute-start(bf16[2,384,256]{1,2,0:T(8,128)(2,1)S(1)} %pad_maximum_fusion.1), channel_id=1, source_target_pairs={{0,4},{4,8},{8,12},{12,16},{16,20},{20,24},{24,28},{1,5},{5,9},{9,... | collective-permute-start | bytes 1179656 | tf_op jit(solution)/shard_map/ppermute | solution.py:16
  17.1 6.5 %collective-permute-done.1 = bf16[2,384,256]{1,2,0:T(8,128)(2,1)S(1)} collective-permute-done((bf16[2,384,256]{1,2,0:T(8,128)(2,1)S(1)}, bf16[2,384,256]{1,2,0:T(8,128)(2,1)S(1)}, u32[]{:S(2)}, u32[]{:S(2)}) %collective-permute-start.1) | collective-permute-done | bytes 393248 | tf_op jit(solution)/shard_map/ppermute | solution.py:17
  23.6 8.6 %collective-permute-done = bf16[2,384,256]{1,2,0:T(8,128)(2,1)S(1)} collective-permute-done((bf16[2,384,256]{1,2,0:T(8,128)(2,1)S(1)}, bf16[2,384,256]{1,2,0:T(8,128)(2,1)S(1)}, u32[]{:S(2)}, u32[]{:S(2)}) %collective-permute-start) | collective-permute-done | bytes 393248 | tf_op jit(solution)/shard_map/ppermute | solution.py:16
  33.3 1.7 %copy.19 = bf16[2,384,6,128]{3,1,2,0:T(8,128)(2,1)S(1)} copy(bf16[2,384,6,128]{1,3,2,0:T(8,128)(2,1)} %bitcast.40) | data formatting | bytes 2359296 | tf_op jit(solution)/shard_map/reshape | solution.py:54
  35.0 2.3 %gather_fusion = bf16[12,2,384,128]{3,2,1,0:T(8,128)(2,1)} fusion(bf16[2,384,6,128]{3,1,2,0:T(8,128)(2,1)S(1)} %copy.19, s32[1024]{0:T(1024)S(1)} %pad_clamp_fusion), kind=kCustom, calls=%fused_computation | custom fusion | bytes 4718640 | tf_op jit(solution)/shard_map/jit(_take)/gather | solution.py:56
  37.4 1.9 %multiply_bitcast_fusion = bf16[2,384,12,128]{3,1,0,2:T(8,128)(2,1)S(1)} fusion(bf16[12,2,384,128]{3,2,1,0:T(8,128)(2,1)} %gather_fusion, pred[12]{0:T(512)(128)(4,1)S(1)} %compare_and_fusion, bf16[12]{0:T(256)(128)(2,1)S(1)} %convert_element_type.25), kind=kLoop, calls=%fused_computation.2 | loop fusion | flops 2359296 | bytes 4718628 | tf_op jit(solution)/shard_map/mul | solution.py:56
  39.4 1.4 %fusion.17 = (bf16[1,384,12,128]{3,1,0,2:T(8,128)(2,1)S(1)}, bf16[1,384,12,128]{3,1,0,2:T(8,128)(2,1)}) fusion(bf16[2,384,12,128]{3,1,0,2:T(8,128)(2,1)S(1)} %multiply_bitcast_fusion), kind=kLoop, calls=%fused_computation.40 | loop fusion | bytes 4718592 | tf_op jit(solution)/shard_map/slice | solution.py:60
  41.1 1.4 %copy.28 = bf16[1,384,12,128]{1,3,2,0:T(8,128)(2,1)} copy(bf16[1,384,12,128]{3,1,0,2:T(8,128)(2,1)S(1)} %get-tuple-element.10) | data formatting | bytes 2359296 | tf_op jit(solution)/shard_map/slice | solution.py:60
  42.5 1.7 %copy.20 = bf16[1,384,12,128]{1,3,2,0:T(8,128)(2,1)S(1)} copy(bf16[1,384,12,128]{3,1,0,2:T(8,128)(2,1)} %get-tuple-element.11) | data formatting | bytes 2359296 | tf_op jit(solution)/shard_map/slice | solution.py:59
  44.2 1.7 %convolution_bitcast_fusion.2 = f32[384,3,128]{2,0,1:T(8,128)S(1)} fusion(bf16[384,3,512]{0,2,1:T(8,128)(2,1)S(1)} %bitcast.34, bf16[3,128,512]{2,1,0:T(8,128)(2,1)} %param.19), kind=kOutput, calls=%fused_computation.8 | convolution fusion | flops 150994944 | bytes 2162688 | tf_op jit(solution)/shard_map/csk,smk->csm/dot_general | solution.py:61
  45.9 1.6 %multiply_reduce_fusion.1 = (f32[3,128]{1,0:T(4,128)S(1)}, f32[384,3,128]{2,0,1:T(8,128)}) fusion(f32[384,3,128]{2,0,1:T(8,128)S(1)} %convolution_bitcast_fusion.2, f32[384]{0:T(512)S(1)} %mul.84, f32[3,128]{1,0:T(4,128)S(1)} %copy-done.9, f32[384]{0:T(512)S(1)} %mul.87, pred[3,128]{1,0:T(4,128)(4,1)S(1)} %iota_compare_fusion.1, ...), kind=kOutput, calls=%fused_computation.11 | convolution fusion | flops 152174208 | bytes 2759040 | tf_op jit(solution)/shard_map/csk,smk->csm/dot_general | solution.py:64
  47.5 1.6 %fusion.16 = f32[3,128,512]{2,1,0:T(8,128)} fusion(bf16[384,3,512]{0,2,1:T(8,128)(2,1)S(1)} %bitcast.48, f32[384,3,128]{2,0,1:T(8,128)S(1)} %convolution_bitcast_fusion.2, f32[384]{0:T(512)S(1)} %mul.84, f32[3,128]{1,0:T(4,128)S(1)} %copy-done.9, f32[384]{0:T(512)S(1)} %mul.87, pred[3,128]{1,0:T(4,128)(4,1)S(1)} %iota_compare_fusion.1), kind=kOutput, calls=%fused_computation.39 | convolution fusion | flops 151879680 | bytes 2560896 | tf_op jit(solution)/shard_map/csm,csk->smk/dot_general | solution.py:106
  49.2 1.5 %copy.24 = bf16[384,3,512]{2,0,1:T(8,128)(2,1)} copy(bf16[384,3,512]{0,2,1:T(8,128)(2,1)S(1)} %bitcast.35) | data formatting | bytes 2359296 | tf_op jit(solution)/shard_map/squeeze | solution.py:59
  50.6 3.0 %fusion = f32[3,128,512]{2,1,0:T(8,128)} fusion(f32[3,128,512]{2,1,0:T(8,128)} %fusion.16, bf16[384,3,512]{0,2,1:T(8,128)(2,1)S(1)} %bitcast.36, f32[384,3,128]{2,0,1:T(8,128)} %get-tuple-element.15, f32[384]{0:T(512)S(1)} %mul.84, f32[3,128]{1,0:T(4,128)S(1)} %copy-done.9, f32[384]{0:T(512)S(1)} %mul.87, pred[3,128]{1,0:T(4,128)(4,1)S(1)} %iota_compare_fusion.1), kind=kOutput, calls=%fused_computation.6 | convolution fusion | flops 152272896 | bytes 3347328 | tf_op jit(solution)/shard_map/csm,csk->smk/dot_general | solution.py:109
  56.4 2.3 %bitcast_subtract_fusion = f32[384,3,512]{2,0,1:T(8,128)} fusion(bf16[384,3,512]{2,0,1:T(8,128)(2,1)S(1)} %copy-done.2, f32[3,384,512]{2,1,0:T(8,128)S(1)} %fusion.19, f32[3,384,512]{2,1,0:T(8,128)S(1)} %fusion.20, bf16[3,128,512]{2,1,0:T(8,128)(2,1)S(1)} %copy-done.4, f32[3,512]{1,0:T(4,128)S(1)} %copy-done.7, f32[384]{0:T(512)S(1)} %mul.87, ...), kind=kOutput, calls=%fused_computation.1 | convolution fusion | flops 156008448 | bytes 9251712 | tf_op jit(solution)/shard_map/csm,smk->csk/dot_general | solution.py:84
  58.7 3.1 %copy.25 = f32[384,3,512]{0,2,1:T(8,128)} copy(f32[384,3,512]{2,0,1:T(8,128)} %bitcast_subtract_fusion) | data formatting | bytes 4718592 | tf_op jit(solution)/shard_map/sub | solution.py:81
  61.8 3.6 %copy.26 = f32[384,12,128]{2,1,0:T(8,128)} copy(f32[384,12,128]{0,2,1:T(8,128)} %bitcast.39) | data formatting | bytes 4718592 | tf_op jit(solution)/shard_map/reshape | solution.py:92
  65.4 3.0 %convolution_bitcast_fusion = f32[384,6,128]{2,1,0:T(8,128)S(1)} fusion(f32[384,12,128]{2,1,0:T(8,128)} %copy.26, s32[12]{0:T(128)S(1)} %eq.15, pred[12]{0:T(512)(128)(4,1)S(1)} %lt.60), kind=kOutput, calls=%fused_computation.4 | convolution fusion | flops 42467472 | bytes 3539004 | tf_op jit(solution)/shard_map/cxb,xw->cwb/dot_general | solution.py:90
  68.5 1.5 %copy.27 = f32[384,6,128]{0,2,1:T(8,128)} copy(f32[384,6,128]{2,1,0:T(8,128)S(1)} %convolution_bitcast_fusion) | data formatting | bytes 2359296 | tf_op jit(solution)/shard_map/cxb,xw->cwb/transpose | solution.py:90
  72.5 5.0 %collective-permute-start.3 = (f32[384,256]{0,1:T(8,128)S(1)}, f32[384,256]{0,1:T(8,128)S(1)}, u32[]{:S(2)}, u32[]{:S(2)}) collective-permute-start(f32[384,256]{0,1:T(8,128)S(1)} %get-tuple-element.13), channel_id=1, source_target_pairs={{0,4},{4,8},{8,12},{12,16},{16,20},{20,24},{24,28},{1,5},{5,9},{9,... | collective-permute-start | bytes 1179656 | tf_op jit(solution)/shard_map/ppermute | solution.py:25
  77.5 2.1 %multiply_reduce_fusion = f32[12,128]{1,0:T(8,128)S(1)} fusion(f32[384]{0:T(512)S(1)} %mul.87, bf16[2,384,12,128]{3,1,0,2:T(8,128)(2,1)} %copy-done.1), kind=kLoop, calls=%fused_computation.3 | loop fusion | flops 2947584 | bytes 2366976 | tf_op jit(solution)/shard_map/reduce_sum | solution.py:73
  79.7 11.6 %all-reduce = (f32[3,128]{1,0:T(4,128)}, f32[3,512]{1,0:T(4,128)}) all-reduce(f32[3,128]{1,0:T(4,128)S(1)} %get-tuple-element.14, f32[3,512]{1,0:T(4,128)S(1)} %neg.11), channel_id=1, replica_groups=mesh['sub'=8,'freq'=4] {'freq'}, use_global_device_ids=true, to_apply=%region_1.2 | all-reduce | flops 1920 | bytes 15360 | tf_op jit(solution)/shard_map/psum | solution.py:79
  91.3 2.1 %collective-permute-done.3 = f32[384,256]{0,1:T(8,128)S(1)} collective-permute-done((f32[384,256]{0,1:T(8,128)S(1)}, f32[384,256]{0,1:T(8,128)S(1)}, u32[]{:S(2)}, u32[]{:S(2)}) %collective-permute-start.3) | collective-permute-done | bytes 393248 | tf_op jit(solution)/shard_map/ppermute | solution.py:25
  (55 shorter events, 11.8 us)
Async XLA Ops:
  7.2 46.5 %copy-start = (bf16[3,512,512]{2,1,0:T(8,128)(2,1)S(1)}, bf16[3,512,512]{2,1,0:T(8,128)(2,1)}, u32[]{:S(2)}) copy-start(bf16[3,512,512]{2,1,0:T(8,128)(2,1)} %param.18) | copy-start | bytes 4718596
  7.2 9.3 %copy-start.8 = (s32[3,4]{1,0:T(4,128)S(1)}, s32[3,4]{1,0:T(4,128)}, u32[]{:S(2)}) copy-start(s32[3,4]{1,0:T(4,128)} %param.14) | copy-start | bytes 148
  7.2 9.5 %copy-start.11 = (s32[3]{0:T(128)S(1)}, s32[3]{0:T(128)}, u32[]{:S(2)}) copy-start(s32[3]{0:T(128)} %param.15) | copy-start | bytes 40
  7.2 9.6 %copy-start.10 = (f32[4]{0:T(128)S(1)}, f32[4]{0:T(128)}, u32[]{:S(2)}) copy-start(f32[4]{0:T(128)} %param.11) | copy-start | bytes 52
  7.2 9.8 %copy-start.12 = (s32[3]{0:T(128)S(1)}, s32[3]{0:T(128)}, u32[]{:S(2)}) copy-start(s32[3]{0:T(128)} %param.16) | copy-start | bytes 40
  7.2 88.2 %reduce-scatter.2.cloned.1.call-start = ((), (), s32[]{:S(2)}) async-start(), calls=%async_computation.1 | async-start | bytes 983040 | tf_op jit(solution)/shard_map/reduce_scatter | solution.py:113
  9.6 14.0 %collective-permute-start.1 = (bf16[2,384,256]{1,2,0:T(8,128)(2,1)S(1)}, bf16[2,384,256]{1,2,0:T(8,128)(2,1)S(1)}, u32[]{:S(2)}, u32[]{:S(2)}) collective-permute-start(bf16[2,384,256]{1,2,0:T(8,128)(2,1)S(1)} %pad_maximum_fusion.1), channel_id=1, source_target_pairs={{4,0},{8,4},{12,8},{16,12},{20,16},{24,20},{28,24},{5,1},{9,5},{13... | collective-permute-start | bytes 1179656 | tf_op jit(solution)/shard_map/ppermute | solution.py:17
  10.9 21.3 %collective-permute-start = (bf16[2,384,256]{1,2,0:T(8,128)(2,1)S(1)}, bf16[2,384,256]{1,2,0:T(8,128)(2,1)S(1)}, u32[]{:S(2)}, u32[]{:S(2)}) collective-permute-start(bf16[2,384,256]{1,2,0:T(8,128)(2,1)S(1)} %pad_maximum_fusion.1), channel_id=1, source_target_pairs={{0,4},{4,8},{8,12},{12,16},{16,20},{20,24},{24,28},{1,5},{5,9},{9,... | collective-permute-start | bytes 1179656 | tf_op jit(solution)/shard_map/ppermute | solution.py:16
  39.4 1.8 %copy-start.1 = (bf16[2,384,12,128]{3,1,0,2:T(8,128)(2,1)}, bf16[2,384,12,128]{3,1,0,2:T(8,128)(2,1)S(1)}, u32[]{:S(2)}) copy-start(bf16[2,384,12,128]{3,1,0,2:T(8,128)(2,1)S(1)} %multiply_bitcast_fusion) | copy-start | bytes 7077892
  44.2 1.7 %copy-start.3 = (bf16[3,128,512]{2,1,0:T(8,128)(2,1)S(1)}, bf16[3,128,512]{2,1,0:T(8,128)(2,1)}, u32[]{:S(2)}) copy-start(bf16[3,128,512]{2,1,0:T(8,128)(2,1)} %param.19) | copy-start | bytes 1179652
  44.2 1.7 %copy-start.6 = (bf16[1,384,12,128]{1,3,2,0:T(8,128)(2,1)S(1)}, bf16[1,384,12,128]{1,3,2,0:T(8,128)(2,1)}, u32[]{:S(2)}) copy-start(bf16[1,384,12,128]{1,3,2,0:T(8,128)(2,1)} %copy.28) | copy-start | bytes 3538948
  44.2 1.7 %copy-start.9 = (f32[3,128]{1,0:T(4,128)S(1)}, f32[3,128]{1,0:T(4,128)}, u32[]{:S(2)}) copy-start(f32[3,128]{1,0:T(4,128)} %param.20) | copy-start | bytes 4612
  53.6 1.4 %copy-start.5 = (bf16[3,512,512]{2,1,0:T(8,128)(2,1)S(1)}, bf16[3,512,512]{2,1,0:T(8,128)(2,1)}, u32[]{:S(2)}) copy-start(bf16[3,512,512]{2,1,0:T(8,128)(2,1)} %param.17) | copy-start | bytes 4718596
  55.0 1.3 %copy-start.2 = (bf16[384,3,512]{2,0,1:T(8,128)(2,1)S(1)}, bf16[384,3,512]{2,0,1:T(8,128)(2,1)}, u32[]{:S(2)}) copy-start(bf16[384,3,512]{2,0,1:T(8,128)(2,1)} %copy.24) | copy-start | bytes 3538948
  55.0 1.3 %copy-start.4 = (bf16[3,128,512]{2,1,0:T(8,128)(2,1)S(1)}, bf16[3,128,512]{2,1,0:T(8,128)(2,1)}, u32[]{:S(2)}) copy-start(bf16[3,128,512]{2,1,0:T(8,128)(2,1)} %param.19) | copy-start | bytes 1179652
  55.0 1.3 %copy-start.7 = (f32[3,512]{1,0:T(4,128)S(1)}, f32[3,512]{1,0:T(4,128)}, u32[]{:S(2)}) copy-start(f32[3,512]{1,0:T(4,128)} %param.21) | copy-start | bytes 18436
  71.2 20.1 %collective-permute-start.2 = (f32[384,256]{0,1:T(8,128)S(1)}, f32[384,256]{0,1:T(8,128)S(1)}, u32[]{:S(2)}, u32[]{:S(2)}) collective-permute-start(f32[384,256]{0,1:T(8,128)S(1)} %get-tuple-element.12), channel_id=1, source_target_pairs={{4,0},{8,4},{12,8},{16,12},{20,16},{24,20},{28,24},{5,1},{9,5},{13... | collective-permute-start | bytes 1179656 | tf_op jit(solution)/shard_map/ppermute | solution.py:25
  72.5 21.0 %collective-permute-start.3 = (f32[384,256]{0,1:T(8,128)S(1)}, f32[384,256]{0,1:T(8,128)S(1)}, u32[]{:S(2)}, u32[]{:S(2)}) collective-permute-start(f32[384,256]{0,1:T(8,128)S(1)} %get-tuple-element.13), channel_id=1, source_target_pairs={{0,4},{4,8},{8,12},{12,16},{16,20},{20,24},{24,28},{1,5},{5,9},{9,... | collective-permute-start | bytes 1179656 | tf_op jit(solution)/shard_map/ppermute | solution.py:25
Sparse Core Ops, SparseCore 0:
  53.7 24.3 reduce-scatter.1
where the time goes:
time: 103 us; the launch traced here: 102 us
  local copies, waits for them, and re-layouts  24.4 us (24%)
  waiting for transfers between devices  17.3 us (17%)
  matrix products  15 us (15%)
  between operations  14.3 us (14%)
  starting transfers between devices  13.2 us (13%)
  blocking collectives  11.6 us (11%)
  other arithmetic  6.49 us (6%)
    psum x1, blocking collectives, shards(): lax.psum((eigen_part, flex_part), 'freq')  11.6 us
    ppermute x1, waiting for transfers between devices, extended(): before = lax.ppermute(last, axis, up)  8.58 us
    ppermute x1, waiting for transfers between devices, extended(): after = lax.ppermute(first, axis, down)  6.51 us
    ppermute x2, starting transfers between devices, from_behind(): return lax.ppermute(block, axis, route)  6.34 us
    ppermute x1, starting transfers between devices, extended(): before = lax.ppermute(last, axis, up)  5.55 us
    unnamed x29, local copies, waits for them, and re-layouts  4.59 us
    reshape x1, local copies, waits for them, and re-layouts, shards(): response.reshape(columns, sub_here * slot_count, block_size)  3.63 us
    sub x1, local copies, waits for them, and re-layouts, shards(): jnp.einsum('csk,sjk->csj', adjoint_sub, stiffness, preferred_element_type...  3.06 us
  transfers between devices with their start and end apart: 5, of which 3 were waited for; matrix products, arithmetic and copies ran while one was open for 21% of the time, Pallas kernels for 0%

commit v1 on v0

v1 whole, which is shorter than its diff:
```python
import functools

import jax
import jax.numpy as jnp
from jax import lax
from jax.experimental import pallas as pl
from jax.experimental.pallas import tpu as pltpu
from jax.sharding import PartitionSpec as P

MESH = pl.DeviceIdType.MESH
NT = (((1,), (1,)), ((), ()))
NN = (((1,), (0,)), ((), ()))
TN = (((0,), (0,)), ((), ()))


def dot(a, b, dims):
    return lax.dot_general(a, b, dims, preferred_element_type=jnp.float32)


def kernel(
    n_sub,
    n_freq,
    chunks,
    freq_ref,
    inc_ref,
    count_ref,
    mode_ref,
    eig_ref,
    flex_ref,
    adj_ref,
    dis_ref,
    stiff_hbm,
    mass_hbm,
    coup_hbm,
    out_ref,
    eig_out,
    cg_out_ref,
    flex_out,
    *scratch,
):
    windows = scratch[:chunks]
    (
        stiff,
        mass,
        coup,
        resp,
        weights,
        picked,
        near_acc,
        far_out,
        far_in,
        near_out,
        near_in,
        pack,
        grad,
        grad_out,
        grad_in,
        own_sem,
        weight_sem,
        near_send,
        near_recv,
        relay_send,
        relay_recv,
        far_send,
        far_recv,
        back_send,
        back_recv,
        pack_send,
        pack_recv,
        grad_send,
        grad_recv,
    ) = scratch[chunks:]
    sub_here, slots = inc_ref.shape
    columns, owned_cells = adj_ref.shape
    rows = columns // chunks
    kb = stiff.shape[1]
    block = kb // slots
    owned = owned_cells // block
    modes = coup.shape[1]
    part = kb // n_freq

    me = lax.axis_index("sub")
    fr = lax.axis_index("freq")
    odd = me % 2
    step = 2 - 4 * odd
    partner = me + 1 - 2 * odd
    target = me + step
    source = me - step
    has_target = (target >= 0) & (target < n_sub)
    has_source = (source >= 0) & (source < n_sub)
    target = jnp.clip(target, 0, n_sub - 1)
    source = jnp.clip(source, 0, n_sub - 1)

    weight_copies = [
        pltpu.make_async_copy(hbm, vmem, weight_sem.at[i])
        for i, (hbm, vmem) in enumerate(((coup_hbm, coup), (stiff_hbm, stiff), (mass_hbm, mass)))
    ]
    own_copies = [
        [
            pltpu.make_async_copy(
                ref.at[pl.ds(c * rows, rows), :], windows[c].at[0, t], own_sem.at[c, t]
            )
            for t, ref in enumerate((adj_ref, dis_ref))
        ]
        for c in range(chunks)
    ]

    def remote(src, dst, send, recv, sub, freq):
        return pltpu.make_async_remote_copy(
            src_ref=src,
            dst_ref=dst,
            send_sem=send,
            recv_sem=recv,
            device_id=(sub, freq),
            device_id_type=MESH,
        )

    near_copies = [
        [
            remote(
                ref.at[pl.ds(c * rows, rows), :],
                windows[c].at[1, t],
                near_send.at[c, t],
                near_recv.at[c, t],
                partner,
                fr,
            )
            for t, ref in enumerate((adj_ref, dis_ref))
        ]
        for c in range(chunks)
    ]
    relay_copies = [
        [
            remote(
                windows[c].at[1, t],
                windows[c].at[2, t],
                relay_send.at[c, t],
                relay_recv.at[c, t],
                target,
                fr,
            )
            for t in range(2)
        ]
        for c in range(chunks)
    ]
    far_copies = [
        remote(far_out.at[c], far_in.at[c], far_send.at[c], far_recv.at[c], source, fr)
        for c in range(chunks)
    ]
    back_copies = [
        remote(near_out.at[c], near_in.at[c], back_send.at[c], back_recv.at[c], partner, fr)
        for c in range(chunks)
    ]
    peers = [(fr + d) % n_freq for d in range(n_freq)]
    pack_copies = [
        remote(pack.at[0], pack.at[d], pack_send.at[d], pack_recv.at[d], me, peers[d])
        for d in range(1, n_freq)
    ]
    grad_copies = [
        [
            remote(
                grad_out.at[s, peers[d]],
                grad_in.at[s, d],
                grad_send.at[s, d],
                grad_recv.at[s, d],
                me,
                peers[d],
            )
            for d in range(1, n_freq)
        ]
        for s in range(sub_here)
    ]

    barrier = pltpu.get_barrier_semaphore()

    def greet(sub, freq):
        pl.semaphore_signal(barrier, inc=1, device_id=(sub, freq), device_id_type=MESH)

    greet(partner, fr)
    for d in range(1, n_freq):
        greet(me, peers[d])

    @pl.when(has_target)
    def _():
        greet(target, fr)

    @pl.when(has_source)
    def _():
        greet(source, fr)

    for copies in own_copies[:1]:
        for copy in copies:
            copy.start()
    for copy in weight_copies:
        copy.start()
    for copies in own_copies[1:]:
        for copy in copies:
            copy.start()

    @pl.when(jnp.logical_not(has_target))
    def _():
        far_in[...] = jnp.zeros_like(far_in)

    pack[0] = jnp.zeros(pack.shape[1:], pack.dtype)
    pl.semaphore_wait(
        barrier, n_freq + has_target.astype(jnp.int32) + has_source.astype(jnp.int32)
    )
    for copies in near_copies:
        for copy in copies:
            copy.start()

    def relay(c):
        for copy in near_copies[c]:
            copy.wait_recv()

        @pl.when(has_target)
        def _():
            for copy in relay_copies[c]:
                copy.start()

    owners = (me, partner, me - 1 + 2 * odd)

    def hits(s, k):
        live = k < count_ref[s]
        named = inc_ref[s, k]
        return [live & (named == owner * owned + inner) for owner in owners for inner in range(owned)]

    def compute(c):
        window = windows[c]
        for copy in own_copies[c]:
            copy.wait()

        @pl.when(has_source)
        def _():
            for copy in relay_copies[c]:
                copy.wait_recv()

        w2 = freq_ref[c]
        w4 = w2 * w2
        base = c * 2 * rows

        def one(s, carry):
            a_parts, d_parts = [], []
            zero = jnp.zeros((rows, block), jnp.bfloat16)
            for k in range(slots):
                a_part, d_part = zero, zero
                for w, hit in enumerate(hits(s, k)):
                    place, inner = w // owned, w % owned
                    lane = pl.ds(inner * block, block)
                    a_part = jnp.where(hit, window[place, 0, :, lane], a_part)
                    d_part = jnp.where(hit, window[place, 1, :, lane], d_part)
                a_parts.append(a_part)
                d_parts.append(d_part)
            a = jnp.concatenate(a_parts, axis=1)
            d = jnp.concatenate(d_parts, axis=1)
            af = a.astype(jnp.float32)
            df = d.astype(jnp.float32)
            picked[s, pl.ds(base, rows), :] = d
            picked[s, pl.ds(base + rows, rows), :] = a
            pack[0, s, 0:1, :] += -w4 * jnp.sum(af * df, axis=0, keepdims=True)
            couple = coup[s]
            ma = dot(a, couple, NT)
            md = dot(d, couple, NT)
            inverse = 1.0 / (eig_ref[pl.ds(s, 1), :] - w2)
            mode_index = lax.broadcasted_iota(jnp.int32, (1, modes), 1)
            factor = jnp.where(mode_index < mode_ref[s], w4 * inverse, 0.0)
            wa = (factor * ma).astype(jnp.bfloat16)
            wd = (factor * md).astype(jnp.bfloat16)
            weights[s, pl.ds(base, rows), :] = wa
            weights[s, pl.ds(base + rows, rows), :] = wd
            pack[0, s, 1:2, 0:modes] += (factor * inverse) * jnp.sum(
                ma * md, axis=0, keepdims=True
            )
            resp[s] = (
                dot(a, stiff[s], NT)
                - w2 * dot(a, mass[s], NT)
                - dot(wa, couple, NN)
                - (w4 * flex_ref[pl.ds(s, 1), :]) * af
            )
            return carry

        if c == 0:
            for copy in weight_copies:
                copy.wait()
        lax.fori_loop(0, sub_here, one, 0)

        places = [
            (s, k, [jnp.where(hit, 1.0, 0.0).astype(jnp.float32) for hit in hits(s, k)])
            for s in range(sub_here)
            for k in range(slots)
        ]
        here = pl.ds(c * rows, rows)
        for place in range(3):
            for inner in range(owned):
                total = None
                for s, k, gains in places:
                    term = gains[place * owned + inner] * resp[s, :, k * block : (k + 1) * block]
                    total = term if total is None else total + term
                lane = pl.ds(inner * block, block)
                if place == 0:
                    out_ref[here, lane] = total
                elif place == 1:
                    near_acc[c, :, lane] = total
                else:
                    far_out[c, :, lane] = total.astype(far_out.dtype)

        @pl.when(has_source)
        def _():
            far_copies[c].start()

    def combine(c):
        @pl.when(has_target)
        def _():
            far_copies[c].wait_recv()

        near_out[c] = (near_acc[c] + far_in[c].astype(jnp.float32)).astype(near_out.dtype)
        back_copies[c].start()

    def finish(c):
        back_copies[c].wait_recv()
        out_ref[pl.ds(c * rows, rows), :] += near_in[c].astype(jnp.float32)

    relay(0)
    for c in range(chunks):
        if c + 1 < chunks:
            relay(c + 1)
        compute(c)
        if c >= 1:
            combine(c - 1)
        if c >= 2:
            finish(c - 2)

    for copy in pack_copies:
        copy.start()

    for s in range(sub_here):
        value = -dot(weights[s], picked[s], TN)
        for j in range(n_freq):
            piece = value[:, j * part : (j + 1) * part]
            grad[s, j] = piece
            grad_out[s, j] = piece.astype(grad_out.dtype)
        for copy in grad_copies[s]:
            copy.start()
        if s == 0:
            combine(chunks - 1)
    if chunks >= 2:
        finish(chunks - 2)

    for copy in pack_copies:
        copy.wait_recv()
    total = None
    for i in range(n_freq):
        term = pack[(fr - i + n_freq) % n_freq]
        total = term if total is None else total + term
    for s in range(sub_here):
        flex_out[s : s + 1, :] = total[s, 0:1, :]
        eig_out[s : s + 1, :] = total[s, 1:2, 0:modes]
    finish(chunks - 1)
    for s in range(sub_here):
        value = grad[s, fr]
        for d in range(1, n_freq):
            grad_copies[s][d - 1].wait_recv()
            value = value + grad_in[s, d].astype(jnp.float32)
        cg_out_ref[s] = value

    for c in range(chunks):
        for copy in near_copies[c]:
            copy.wait_send()
        back_copies[c].wait_send()

    @pl.when(has_target)
    def _():
        for c in range(chunks):
            for copy in relay_copies[c]:
                copy.wait_send()

    @pl.when(has_source)
    def _():
        for c in range(chunks):
            far_copies[c].wait_send()

    for copy in pack_copies:
        copy.wait_send()
    for s in range(sub_here):
        for copy in grad_copies[s]:
            copy.wait_send()


def shards(
    n_sub,
    n_freq,
    freq_squared,
    displacement,
    adjoint,
    incidence,
    block_count,
    mode_count,
    stiffness,
    mass_matrix,
    coupling,
    eigenvalues,
    flexibility,
):
    sub_here = incidence.shape[0]
    columns, owned_cells = displacement.shape
    chunks = freq_squared.shape[0]
    rows = columns // chunks
    kb = stiffness.shape[1]
    modes = coupling.shape[1]
    part = kb // n_freq
    bf16, f32 = jnp.bfloat16, jnp.float32
    smem = pl.BlockSpec(memory_space=pltpu.SMEM)
    vmem = pl.BlockSpec(memory_space=pltpu.VMEM)
    anywhere = pl.BlockSpec(memory_space=pl.ANY)
    dma = pltpu.SemaphoreType.DMA
    slab = (chunks, rows, owned_cells)
    scratch = [pltpu.VMEM((3, 2, rows, owned_cells), bf16) for _ in range(chunks)] + [
        pltpu.VMEM(stiffness.shape, bf16),
        pltpu.VMEM(mass_matrix.shape, bf16),
        pltpu.VMEM(coupling.shape, bf16),
        pltpu.VMEM((sub_here, rows, kb), f32),
        pltpu.VMEM((sub_here, 2 * columns, modes), bf16),
        pltpu.VMEM((sub_here, 2 * columns, kb), bf16),
        pltpu.VMEM(slab, f32),
        pltpu.VMEM(slab, bf16),
        pltpu.VMEM(slab, bf16),
        pltpu.VMEM(slab, bf16),
        pltpu.VMEM(slab, bf16),
        pltpu.VMEM((n_freq, sub_here, 8, kb), f32),
        pltpu.VMEM((sub_here, n_freq, modes, part), f32),
        pltpu.VMEM((sub_here, n_freq, modes, part), bf16),
        pltpu.VMEM((sub_here, n_freq, modes, part), bf16),
        dma((chunks, 2)),
        dma((3,)),
        dma((chunks, 2)),
        dma((chunks, 2)),
        dma((chunks, 2)),
        dma((chunks, 2)),
        dma((chunks,)),
        dma((chunks,)),
        dma((chunks,)),
        dma((chunks,)),
        dma((n_freq,)),
        dma((n_freq,)),
        dma((sub_here, n_freq)),
        dma((sub_here, n_freq)),
    ]
    return pl.pallas_call(
        functools.partial(kernel, n_sub, n_freq, chunks),
        out_shape=(
            jax.ShapeDtypeStruct((columns, owned_cells), f32),
            jax.ShapeDtypeStruct((sub_here, modes), f32),
            jax.ShapeDtypeStruct((sub_here, modes, part), f32),
            jax.ShapeDtypeStruct((sub_here, kb), f32),
        ),
        in_specs=[smem] * 4 + [vmem] * 2 + [anywhere] * 5,
        out_specs=(vmem,) * 4,
        scratch_shapes=scratch,
        compiler_params=pltpu.CompilerParams(
            collective_id=0, has_side_effects=True, vmem_limit_bytes=48 * 1024 * 1024
        ),
    )(
        freq_squared,
        incidence,
        block_count,
        mode_count,
        eigenvalues,
        flexibility,
        adjoint,
        displacement,
        stiffness,
        mass_matrix,
        coupling,
    )


def solution(mesh):
    in_specs = (
        P("freq"),
        P("freq", "sub"),
        P("freq", "sub"),
        P("sub", None),
        P("sub"),
        P("sub"),
        P("sub", None, None),
        P("sub", None, None),
        P("sub", None, None),
        P("sub", None),
        P("sub", None),
    )
    out_specs = (P("freq", "sub"), P("sub", None), P("sub", None, "freq"), P("sub", None))
    body = functools.partial(shards, mesh.shape["sub"], mesh.shape["freq"])
    return jax.shard_map(body, mesh=mesh, in_specs=in_specs, out_specs=out_specs, check_vma=False)
```

time: 103 us -> 45.1 us (0.44)
  Pallas kernels: 0 us -> 31.8 us
  waiting for transfers between devices: 17.3 us -> 0 us
  matrix products: 15 us -> 0 us
  between operations: 14.3 us -> 0.66 us
  starting transfers between devices: 13.2 us -> 0 us
  local copies, waits for them, and re-layouts: 24.4 us -> 12.3 us
  blocking collectives: 11.6 us -> 0 us
  other arithmetic: 6.49 us -> 0 us
    pallas_call x0 -> x1, Pallas kernels: none -> 31.8 us  [shards(): pl.pallas_call(functools.partial(kernel, n_sub, n_freq, chunks), out_shap...]
    ppermute x4 -> x0, waiting for transfers between devices: 17.2 us -> none  [the longest x1 8.58 us: extended(): before = lax.ppermute(last, axis, up)]
    dot_general x8 -> x0, matrix products: 15 us -> none  [the longest x1 3.04 us: shards(): jnp.einsum('cxb,xw->cwb', response.reshape(columns, sub_here * slot_count...]
    ppermute x4 -> x0, starting transfers between devices: 13.2 us -> none  [the longest x2 6.34 us: from_behind(): return lax.ppermute(block, axis, route)]
    psum x1 -> x0, blocking collectives: 11.6 us -> none  [shards(): lax.psum((eigen_part, flex_part), 'freq')]
    unnamed x29 -> x26, local copies, waits for them, and re-layouts: 4.59 us -> 12.3 us
    slice x4 -> x0, local copies, waits for them, and re-layouts: 5.68 us -> none  [the longest x2 2.75 us: shards(): displacement_sub = picked[1]]
    reshape x3 -> x0, local copies, waits for them, and re-layouts: 5.4 us -> none  [the longest x1 3.63 us: shards(): response.reshape(columns, sub_here * slot_count, block_size)]
  transfers between devices with their start and end apart: 5 -> 0, of which waited for: 3 -> 0; matrix products, arithmetic and copies ran while one was open for 21% -> 0% of each run, Pallas kernels for 0% -> 0%
where the time goes in v1:
time: 45.1 us; the launch traced here: 44.7 us
  Pallas kernels  31.8 us (71%)
  local copies, waits for them, and re-layouts  12.3 us (27%)
  between operations  0.66 us (1%)
    pallas_call x1, Pallas kernels, shards(): pl.pallas_call(functools.partial(kernel, n_sub, n_freq, chunks), out_shap...  31.8 us
    unnamed x26, local copies, waits for them, and re-layouts  12.3 us

profile of v1, /device:TPU:0, one launch (start us, length us, event | category | flops | bytes accessed | tf_op | source)
XLA Modules:
  0.0 44.7 jit_solution(17423137958621086690)
XLA Ops:
  0.6 0.0 copy-start
  0.6 1.4 %copy-done = bf16[3,512,512]{2,1,0:T(8,128)(2,1)S(1)} copy-done((bf16[3,512,512]{2,1,0:T(8,128)(2,1)S(1)}, bf16[3,512,512]{2,1,0:T(8,128)(2,1)}, u32[]{:S(2)}) %copy-start) | copy-done | bytes 1572888
  2.0 0.0 copy-start.1
  2.0 1.4 %copy-done.1 = bf16[3,512,512]{2,1,0:T(8,128)(2,1)S(1)} copy-done((bf16[3,512,512]{2,1,0:T(8,128)(2,1)S(1)}, bf16[3,512,512]{2,1,0:T(8,128)(2,1)}, u32[]{:S(2)}) %copy-start.1) | copy-done | bytes 1572888
  3.5 0.0 copy-start.2
  3.5 1.0 %copy-done.2 = bf16[3,128,512]{2,1,0:T(8,128)(2,1)S(1)} copy-done((bf16[3,128,512]{2,1,0:T(8,128)(2,1)S(1)}, bf16[3,128,512]{2,1,0:T(8,128)(2,1)}, u32[]{:S(2)}) %copy-start.2) | copy-done | bytes 393240
  4.4 0.0 copy-start.3
  4.5 0.9 %copy-done.3 = bf16[384,256]{1,0:T(8,128)(2,1)S(1)} copy-done((bf16[384,256]{1,0:T(8,128)(2,1)S(1)}, bf16[384,256]{1,0:T(8,128)(2,1)}, u32[]{:S(2)}) %copy-start.3) | copy-done | bytes 196632
  5.4 0.0 copy-start.4
  5.4 0.9 %copy-done.4 = bf16[384,256]{1,0:T(8,128)(2,1)S(1)} copy-done((bf16[384,256]{1,0:T(8,128)(2,1)S(1)}, bf16[384,256]{1,0:T(8,128)(2,1)}, u32[]{:S(2)}) %copy-start.4) | copy-done | bytes 196632
  6.3 0.0 copy-start.5
  6.3 0.7 %copy-done.5 = f32[3,512]{1,0:T(4,128)S(1)} copy-done((f32[3,512]{1,0:T(4,128)S(1)}, f32[3,512]{1,0:T(4,128)}, u32[]{:S(2)}) %copy-start.5) | copy-done | bytes 6168
  7.0 0.0 copy-start.6
  7.0 0.7 %copy-done.6 = s32[3,4]{1,0:T(4,128)S(1)} copy-done((s32[3,4]{1,0:T(4,128)S(1)}, s32[3,4]{1,0:T(4,128)}, u32[]{:S(2)}) %copy-start.6) | copy-done | bytes 72
  7.7 0.0 copy-start.7
  7.7 0.7 %copy-done.7 = f32[3,128]{1,0:T(4,128)S(1)} copy-done((f32[3,128]{1,0:T(4,128)S(1)}, f32[3,128]{1,0:T(4,128)}, u32[]{:S(2)}) %copy-start.7) | copy-done | bytes 1560
  8.4 0.7 %copy-done.8 = f32[4]{0:T(128)S(1)} copy-done((f32[4]{0:T(128)S(1)}, f32[4]{0:T(128)}, u32[]{:S(2)}) %copy-start.8) | copy-done | bytes 40
  9.0 0.7 %copy-done.9 = s32[3]{0:T(128)S(1)} copy-done((s32[3]{0:T(128)S(1)}, s32[3]{0:T(128)}, u32[]{:S(2)}) %copy-start.9) | copy-done | bytes 36
  9.7 0.7 %copy-done.10 = s32[3]{0:T(128)S(1)} copy-done((s32[3]{0:T(128)S(1)}, s32[3]{0:T(128)}, u32[]{:S(2)}) %copy-start.10) | copy-done | bytes 36
  10.3 31.8 %shard_map.138 = (f32[384,256]{1,0:T(8,128)S(1)}, f32[3,128]{1,0:T(4,128)S(1)}, f32[3,128,128]{2,1,0:T(8,128)S(1)}, f32[3,512]{1,0:T(4,128)S(1)}) custom-call(f32[4]{0:T(128)S(1)} %copy-done.8, s32[3,4]{1,0:T(4,128)S(1)} %copy-done.6, s32[3]{0:T(128)S(1)} %copy-done.9, s32[3]{0:T(128)S(1)} %copy-done.10, f32[3,128]{1,0:T(4,128)S(1)} %copy-done.7, ...), custom_call_target="tpu_custom_call" | custom-call | tf_op jit(solution)/shard_map/pallas_call | solution.py:448
  42.1 0.7 %copy.19 = f32[384,256]{1,0:T(8,128)} copy(f32[384,256]{1,0:T(8,128)S(1)} %get-tuple-element.8) | data formatting | bytes 786432
  42.9 0.6 %copy.20 = f32[3,128]{1,0:T(4,128)} copy(f32[3,128]{1,0:T(4,128)S(1)} %get-tuple-element.9) | data formatting | bytes 3072
  43.5 0.7 %copy.21 = f32[3,128,128]{2,1,0:T(8,128)} copy(f32[3,128,128]{2,1,0:T(8,128)S(1)} %get-tuple-element.10) | data formatting | bytes 393216
  44.1 0.6 %copy.22 = f32[3,512]{1,0:T(4,128)} copy(f32[3,512]{1,0:T(4,128)S(1)} %get-tuple-element.11) | data formatting | bytes 12288
  (3 shorter events, 0.0 us)
Async XLA Ops:
  0.6 1.4 %copy-start = (bf16[3,512,512]{2,1,0:T(8,128)(2,1)S(1)}, bf16[3,512,512]{2,1,0:T(8,128)(2,1)}, u32[]{:S(2)}) copy-start(bf16[3,512,512]{2,1,0:T(8,128)(2,1)} %stiff_hbm.1) | copy-start | bytes 4718596
  2.0 1.4 %copy-start.1 = (bf16[3,512,512]{2,1,0:T(8,128)(2,1)S(1)}, bf16[3,512,512]{2,1,0:T(8,128)(2,1)}, u32[]{:S(2)}) copy-start(bf16[3,512,512]{2,1,0:T(8,128)(2,1)} %mass_hbm.1) | copy-start | bytes 4718596
  3.5 1.0 %copy-start.2 = (bf16[3,128,512]{2,1,0:T(8,128)(2,1)S(1)}, bf16[3,128,512]{2,1,0:T(8,128)(2,1)}, u32[]{:S(2)}) copy-start(bf16[3,128,512]{2,1,0:T(8,128)(2,1)} %coup_hbm.1) | copy-start | bytes 1179652
  4.4 0.9 %copy-start.3 = (bf16[384,256]{1,0:T(8,128)(2,1)S(1)}, bf16[384,256]{1,0:T(8,128)(2,1)}, u32[]{:S(2)}) copy-start(bf16[384,256]{1,0:T(8,128)(2,1)} %adj_ref.1) | copy-start | bytes 589828
  5.4 0.9 %copy-start.4 = (bf16[384,256]{1,0:T(8,128)(2,1)S(1)}, bf16[384,256]{1,0:T(8,128)(2,1)}, u32[]{:S(2)}) copy-start(bf16[384,256]{1,0:T(8,128)(2,1)} %dis_ref.1) | copy-start | bytes 589828
  6.3 0.7 %copy-start.5 = (f32[3,512]{1,0:T(4,128)S(1)}, f32[3,512]{1,0:T(4,128)}, u32[]{:S(2)}) copy-start(f32[3,512]{1,0:T(4,128)} %flex_ref.1) | copy-start | bytes 18436
  7.0 0.7 %copy-start.6 = (s32[3,4]{1,0:T(4,128)S(1)}, s32[3,4]{1,0:T(4,128)}, u32[]{:S(2)}) copy-start(s32[3,4]{1,0:T(4,128)} %inc_ref.1) | copy-start | bytes 148
  7.7 0.7 %copy-start.7 = (f32[3,128]{1,0:T(4,128)S(1)}, f32[3,128]{1,0:T(4,128)}, u32[]{:S(2)}) copy-start(f32[3,128]{1,0:T(4,128)} %eig_ref.1) | copy-start | bytes 4612
  8.4 0.7 %copy-start.8 = (f32[4]{0:T(128)S(1)}, f32[4]{0:T(128)}, u32[]{:S(2)}) copy-start(f32[4]{0:T(128)} %freq_ref.1) | copy-start | bytes 52
  9.0 0.7 %copy-start.9 = (s32[3]{0:T(128)S(1)}, s32[3]{0:T(128)}, u32[]{:S(2)}) copy-start(s32[3]{0:T(128)} %count_ref.1) | copy-start | bytes 40
  9.7 0.7 %copy-start.10 = (s32[3]{0:T(128)S(1)}, s32[3]{0:T(128)}, u32[]{:S(2)}) copy-start(s32[3]{0:T(128)} %mode_ref.1) | copy-start | bytes 40

commit v2 on v1

--- a/solution.py
+++ b/solution.py
@@ -21,12 +21,12 @@
     n_sub,
     n_freq,
     chunks,
-    freq_ref,
-    inc_ref,
-    count_ref,
-    mode_ref,
-    eig_ref,
-    flex_ref,
+    freq_hbm,
+    inc_hbm,
+    count_hbm,
+    mode_hbm,
+    eig_hbm,
+    flex_hbm,
     adj_ref,
     dis_ref,
     stiff_hbm,
@@ -40,6 +40,12 @@
 ):
     windows = scratch[:chunks]
     (
+        freq_ref,
+        inc_ref,
+        count_ref,
+        mode_ref,
+        eig_ref,
+        flex_ref,
         stiff,
         mass,
         coup,
@@ -57,6 +63,7 @@
         grad_in,
         own_sem,
         weight_sem,
+        small_sem,
         near_send,
         near_recv,
         relay_send,
@@ -95,6 +102,19 @@
         pltpu.make_async_copy(hbm, vmem, weight_sem.at[i])
         for i, (hbm, vmem) in enumerate(((coup_hbm, coup), (stiff_hbm, stiff), (mass_hbm, mass)))
     ]
+    small_copies = [
+        pltpu.make_async_copy(hbm, local, small_sem.at[i])
+        for i, (hbm, local) in enumerate(
+            (
+                (freq_hbm, freq_ref),
+                (inc_hbm, inc_ref),
+                (count_hbm, count_ref),
+                (mode_hbm, mode_ref),
+                (eig_hbm, eig_ref),
+                (flex_hbm, flex_ref),
+            )
+        )
+    ]
     own_copies = [
         [
             pltpu.make_async_copy(
@@ -188,6 +208,8 @@
     def _():
         greet(source, fr)
 
+    for copy in small_copies:
+        copy.start()
     for copies in own_copies[:1]:
         for copy in copies:
             copy.start()
@@ -235,6 +257,9 @@
             for copy in relay_copies[c]:
                 copy.wait_recv()
 
+        if c == 0:
+            for copy in small_copies + weight_copies:
+                copy.wait()
         w2 = freq_ref[c]
         w4 = w2 * w2
         base = c * 2 * rows
@@ -279,9 +304,6 @@
             )
             return carry
 
-        if c == 0:
-            for copy in weight_copies:
-                copy.wait()
         lax.fori_loop(0, sub_here, one, 0)
 
         places = [
@@ -409,12 +431,17 @@
     modes = coupling.shape[1]
     part = kb // n_freq
     bf16, f32 = jnp.bfloat16, jnp.float32
-    smem = pl.BlockSpec(memory_space=pltpu.SMEM)
     vmem = pl.BlockSpec(memory_space=pltpu.VMEM)
-    anywhere = pl.BlockSpec(memory_space=pl.ANY)
+    hbm = pl.BlockSpec(memory_space=pltpu.HBM)
     dma = pltpu.SemaphoreType.DMA
     slab = (chunks, rows, owned_cells)
     scratch = [pltpu.VMEM((3, 2, rows, owned_cells), bf16) for _ in range(chunks)] + [
+        pltpu.SMEM(freq_squared.shape, f32),
+        pltpu.SMEM(incidence.shape, jnp.int32),
+        pltpu.SMEM(block_count.shape, jnp.int32),
+        pltpu.SMEM(mode_count.shape, jnp.int32),
+        pltpu.VMEM(eigenvalues.shape, f32),
+        pltpu.VMEM(flexibility.shape, f32),
         pltpu.VMEM(stiffness.shape, bf16),
         pltpu.VMEM(mass_matrix.shape, bf16),
         pltpu.VMEM(coupling.shape, bf16),
@@ -432,6 +459,7 @@
         pltpu.VMEM((sub_here, n_freq, modes, part), bf16),
         dma((chunks, 2)),
         dma((3,)),
+        dma((6,)),
         dma((chunks, 2)),
         dma((chunks, 2)),
         dma((chunks, 2)),
@@ -453,11 +481,11 @@
             jax.ShapeDtypeStruct((sub_here, modes, part), f32),
             jax.ShapeDtypeStruct((sub_here, kb), f32),
         ),
-        in_specs=[smem] * 4 + [vmem] * 2 + [anywhere] * 5,
+        in_specs=[hbm] * 11,
         out_specs=(vmem,) * 4,
         scratch_shapes=scratch,
         compiler_params=pltpu.CompilerParams(
-            collective_id=0, has_side_effects=True, vmem_limit_bytes=48 * 1024 * 1024
+            collective_id=0, has_side_effects=True, vmem_limit_bytes=67043328
         ),
     )(
         freq_squared,

time: 45.1 us -> 39.2 us (0.87)
  local copies, waits for them, and re-layouts: 12.3 us -> 5.92 us
  Pallas kernels: 31.8 us -> 32.4 us
    unnamed x26 -> x4, local copies, waits for them, and re-layouts: 12.3 us -> 5.92 us
    pallas_call x1, Pallas kernels: 31.8 us -> 32.4 us  [shards(): pl.pallas_call(functools.partial(kernel, n_sub, n_freq, chunks), out_shap...]
where the time goes in v2:
time: 39.2 us; the launch traced here: 38.9 us
  Pallas kernels  32.4 us (83%)
  local copies, waits for them, and re-layouts  5.92 us (15%)
  between operations  0.64 us (2%)
    pallas_call x1, Pallas kernels, shards(): pl.pallas_call(functools.partial(kernel, n_sub, n_freq, chunks), out_shap...  32.4 us
    unnamed x4, local copies, waits for them, and re-layouts  5.92 us

profile of v2, /device:TPU:0, one launch (start us, length us, event | category | flops | bytes accessed | tf_op | source)
XLA Modules:
  0.0 38.9 jit_solution(17569469239380605296)
XLA Ops:
  0.6 32.4 %shard_map.138 = (f32[384,256]{1,0:T(8,128)}, f32[3,128]{1,0:T(4,128)}, f32[3,128,128]{2,1,0:T(8,128)}, f32[3,512]{1,0:T(4,128)}) custom-call(f32[4]{0:T(128)} %freq_hbm.1, s32[3,4]{1,0:T(4,128)} %inc_hbm.1, s32[3]{0:T(128)} %count_hbm.1, s32[3]{0:T(128)} %mode_hbm.1, f32[3,128]{1,0:T(4,128)} %eig_hbm.1, f32[3,512]{1,0:T(4,128)} %flex_hbm.1, ...), custom_call_target="tpu_custom_call" | custom-call | tf_op jit(solution)/shard_map/pallas_call | solution.py:476
  33.0 1.8 %copy.19 = f32[384,256]{1,0:T(8,128)} copy(f32[384,256]{1,0:T(8,128)} %get-tuple-element.8) | data formatting | bytes 786432
  34.8 1.2 %copy.20 = f32[3,128]{1,0:T(4,128)} copy(f32[3,128]{1,0:T(4,128)} %get-tuple-element.9) | data formatting | bytes 3072
  36.0 1.6 %copy.21 = f32[3,128,128]{2,1,0:T(8,128)} copy(f32[3,128,128]{2,1,0:T(8,128)} %get-tuple-element.10) | data formatting | bytes 393216
  37.6 1.3 %copy.22 = f32[3,512]{1,0:T(4,128)} copy(f32[3,512]{1,0:T(4,128)} %get-tuple-element.11) | data formatting | bytes 12288

commit v3 on v2

--- a/solution.py
+++ b/solution.py
@@ -408,6 +408,18 @@
             copy.wait_send()
 
 
+def write_out(*refs):
+    count = len(refs) // 2
+    sems = refs[-1]
+    copies = [
+        pltpu.make_async_copy(refs[i], refs[count + i], sems.at[i]) for i in range(count)
+    ]
+    for copy in copies:
+        copy.start()
+    for copy in copies:
+        copy.wait()
+
+
 def shards(
     n_sub,
     n_freq,
@@ -473,7 +485,7 @@
         dma((sub_here, n_freq)),
         dma((sub_here, n_freq)),
     ]
-    return pl.pallas_call(
+    results = pl.pallas_call(
         functools.partial(kernel, n_sub, n_freq, chunks),
         out_shape=(
             jax.ShapeDtypeStruct((columns, owned_cells), f32),
@@ -485,21 +497,34 @@
         out_specs=(vmem,) * 4,
         scratch_shapes=scratch,
         compiler_params=pltpu.CompilerParams(
-            collective_id=0, has_side_effects=True, vmem_limit_bytes=67043328
+            collective_id=0, has_side_effects=True, vmem_limit_bytes=48 * 1024 * 1024
         ),
     )(
-        freq_squared,
-        incidence,
-        block_count,
-        mode_count,
-        eigenvalues,
-        flexibility,
-        adjoint,
-        displacement,
-        stiffness,
-        mass_matrix,
-        coupling,
+        *(
+            pltpu.with_memory_space_constraint(x, pltpu.HBM)
+            for x in (
+                freq_squared,
+                incidence,
+                block_count,
+                mode_count,
+                eigenvalues,
+                flexibility,
+                adjoint,
+                displacement,
+                stiffness,
+                mass_matrix,
+                coupling,
+            )
+        )
     )
+    return pl.pallas_call(
+        write_out,
+        out_shape=tuple(jax.ShapeDtypeStruct(x.shape, x.dtype) for x in results),
+        in_specs=[vmem] * 4,
+        out_specs=(pl.BlockSpec(memory_space=pltpu.HBM),) * 4,
+        scratch_shapes=[dma((4,))],
+        compiler_params=pltpu.CompilerParams(vmem_limit_bytes=4 * 1024 * 1024),
+    )(*results)
 
 
 def solution(mesh):

time: 39.2 us -> 33.2 us (0.85)
  local copies, waits for them, and re-layouts: 5.92 us -> 0 us
    unnamed x4 -> x0, local copies, waits for them, and re-layouts: 5.92 us -> none
    pallas_call x0 -> x1, Pallas kernels: none -> 0.85 us  [shards(): pl.pallas_call(write_out, out_shape=tuple((jax.ShapeDtypeStruct(x.shape,...]
    pallas_call x1, Pallas kernels: 32.4 us -> 31.6 us  [shards(): pl.pallas_call(functools.partial(kernel, n_sub, n_freq, chunks), out_shap...]
where the time goes in v3:
time: 33.2 us; the launch traced here: 33.1 us
  Pallas kernels  32.4 us (98%)
  between operations  0.64 us (2%)
    pallas_call x1, Pallas kernels, shards(): pl.pallas_call(functools.partial(kernel, n_sub, n_freq, chunks), out_shap...  31.6 us
    pallas_call x1, Pallas kernels, shards(): pl.pallas_call(write_out, out_shape=tuple((jax.ShapeDtypeStruct(x.shape,...  0.85 us

profile of v3, /device:TPU:0, one launch (start us, length us, event | category | flops | bytes accessed | tf_op | source)
XLA Modules:
  0.0 33.1 jit_solution(12920267774864755868)
XLA Ops:
  0.6 31.6 %shard_map.138 = (f32[384,256]{1,0:T(8,128)S(1)}, f32[3,128]{1,0:T(4,128)S(1)}, f32[3,128,128]{2,1,0:T(8,128)S(1)}, f32[3,512]{1,0:T(4,128)S(1)}) custom-call(f32[4]{0:T(128)} %freq_hbm.1, s32[3,4]{1,0:T(4,128)} %inc_hbm.1, s32[3]{0:T(128)} %count_hbm.1, s32[3]{0:T(128)} %mode_hbm.1, f32[3,128]{1,0:T(4,128)} %eig_hbm.1, f32[3,512]{1,0:T(4,128)} %flex_hbm.1, ...), custom_call_target="tpu_custom_call" | custom-call | tf_op jit(solution)/shard_map/pallas_call | solution.py:488
  32.2 0.8 %shard_map.139 = (f32[384,256]{1,0:T(8,128)}, f32[3,128]{1,0:T(4,128)}, f32[3,128,128]{2,1,0:T(8,128)}, f32[3,512]{1,0:T(4,128)}) custom-call(f32[384,256]{1,0:T(8,128)S(1)} %get-tuple-element.8.refs_0_, f32[3,128]{1,0:T(4,128)S(1)} %get-tuple-element.9.refs_1_, f32[3,128,128]{2,1,0:T(8,128)S(1)} %get-tuple-element.10.refs_2_, ...), custom_call_target="tpu_custom_call" | custom-call | tf_op jit(solution)/shard_map/pallas_call | solution.py:520

commit v4 on v3

--- a/solution.py
+++ b/solution.py
@@ -312,7 +312,7 @@
             for k in range(slots)
         ]
         here = pl.ds(c * rows, rows)
-        for place in range(3):
+        for place in (2, 1, 0):
             for inner in range(owned):
                 total = None
                 for s, k, gains in places:
@@ -326,9 +326,11 @@
                 else:
                     far_out[c, :, lane] = total.astype(far_out.dtype)
 
-        @pl.when(has_source)
-        def _():
-            far_copies[c].start()
+            if place == 2:
+
+                @pl.when(has_source)
+                def _():
+                    far_copies[c].start()
 
     def combine(c):
         @pl.when(has_target)
@@ -347,10 +349,8 @@
         if c + 1 < chunks:
             relay(c + 1)
         compute(c)
-        if c >= 1:
-            combine(c - 1)
         if c >= 2:
-            finish(c - 2)
+            combine(c - 2)
 
     for copy in pack_copies:
         copy.start()
@@ -363,10 +363,10 @@
             grad_out[s, j] = piece.astype(grad_out.dtype)
         for copy in grad_copies[s]:
             copy.start()
-        if s == 0:
-            combine(chunks - 1)
-    if chunks >= 2:
-        finish(chunks - 2)
+    for c in range(max(chunks - 2, 0), chunks):
+        combine(c)
+    for c in range(chunks - 1):
+        finish(c)
 
     for copy in pack_copies:
         copy.wait_recv()

time: 33.2 us -> 31.1 us (0.937)
  Pallas kernels: 32.4 us -> 30.3 us
    pallas_call x1, Pallas kernels: 31.6 us -> 29.5 us  [shards(): pl.pallas_call(functools.partial(kernel, n_sub, n_freq, chunks), out_shap...]
where the time goes in v4:
time: 31.1 us; the launch traced here: 30.9 us
  Pallas kernels  30.3 us (97%)
  between operations  0.64 us (2%)
    pallas_call x1, Pallas kernels, shards(): pl.pallas_call(functools.partial(kernel, n_sub, n_freq, chunks), out_shap...  29.5 us
    pallas_call x1, Pallas kernels, shards(): pl.pallas_call(write_out, out_shape=tuple((jax.ShapeDtypeStruct(x.shape,...  0.85 us

profile of v4, /device:TPU:0, one launch (start us, length us, event | category | flops | bytes accessed | tf_op | source)
XLA Modules:
  0.0 30.9 jit_solution(4125307584840178514)
XLA Ops:
  0.6 29.5 %shard_map.138 = (f32[384,256]{1,0:T(8,128)S(1)}, f32[3,128]{1,0:T(4,128)S(1)}, f32[3,128,128]{2,1,0:T(8,128)S(1)}, f32[3,512]{1,0:T(4,128)S(1)}) custom-call(f32[4]{0:T(128)} %freq_hbm.1, s32[3,4]{1,0:T(4,128)} %inc_hbm.1, s32[3]{0:T(128)} %count_hbm.1, s32[3]{0:T(128)} %mode_hbm.1, f32[3,128]{1,0:T(4,128)} %eig_hbm.1, f32[3,512]{1,0:T(4,128)} %flex_hbm.1, ...), custom_call_target="tpu_custom_call" | custom-call | tf_op jit(solution)/shard_map/pallas_call | solution.py:488
  30.1 0.8 %shard_map.139 = (f32[384,256]{1,0:T(8,128)}, f32[3,128]{1,0:T(4,128)}, f32[3,128,128]{2,1,0:T(8,128)}, f32[3,512]{1,0:T(4,128)}) custom-call(f32[384,256]{1,0:T(8,128)S(1)} %get-tuple-element.8.refs_0_, f32[3,128]{1,0:T(4,128)S(1)} %get-tuple-element.9.refs_1_, f32[3,128,128]{2,1,0:T(8,128)S(1)} %get-tuple-element.10.refs_2_, ...), custom_call_target="tpu_custom_call" | custom-call | tf_op jit(solution)/shard_map/pallas_call | solution.py:520
